TPU v7x, 256 devices: a whole 4x4x8 slice. The times are simulated.
256 devices in a mesh: row: 32 (over x, z), feat: 8 (over y, core).
Axes of the slice: x: 4, y: 4, z: 8, core: 2. Of those that a mesh axis runs over, the one named last changes fastest.
Arguments:
- predictor: float32 [131072], P(('row', 'feat')), may hold values from -3 to 3
- events: int32 [131072], P(('row', 'feat')), may hold values 0 or 1
- tie_groups: int32 [131072], P(('row', 'feat')), may hold values from 7 to 131071, as said below
- node_ids: int32 [131072], P('row'), may hold values from 0 to 7
- bin_index: int32 [512, 131072], P('feat', 'row'), may hold values from 0 to 255
Outputs:
- gradient: float32 [131072], P(('row', 'feat'))
- hessian: float32 [131072], P(('row', 'feat'))
- split_gain: float32 [8, 512, 256], P(None, 'feat', 'row')
Inputs may be any that keep to these rules, and one draw needn't show every extreme that they name: tie_groups never falls along the rows; each value names a run of 1 to 8 consecutive rows, some run has exactly 8, and a new run begins at every multiple of 8 rows.
All inputs are finite; a program needn't handle non-finite values. No bound on the sum of `events` on one device may be relied on, other than what follows from the above.
Results may differ from a plain program's by a relative error of at most 0.0003.
The roundings to bfloat16 on the way count: a program that leaves them out, or rounds other values in their place, can miss the bound.
Values may be sent and summed in bfloat16 or wider, within the bound.
No kernel may reach another device: no remote copies, remote signals or barrier semaphores. Data moves between devices by JAX's collectives and lax.ppermute only.
A program may use at most 64 MiB of HBM per device.

v0:
```python
import math

import jax
import jax.numpy as jnp
from jax import lax
from jax.sharding import Mesh
from jax.sharding import PartitionSpec as P

BINS = 256
NODES = 8
ROW_FEAT = ("row_0", "row_1", "feat_0", "feat_1")
FEAT = ("feat_0", "feat_1")
ROW = ("row_0", "row_1")


def neutral_like(shard, identity):
    return jax.tree.map(
        lambda a, e: jnp.broadcast_to(jnp.asarray(e, a.dtype), a.shape), shard, identity
    )


def entering(shard, axes, combine, identity):
    before = start = neutral_like(shard, identity)
    subtotal = shard
    for axis in reversed(axes):
        size, position = (lax.axis_size(axis), lax.axis_index(axis))
        pieces = lax.all_gather(subtotal, axis)
        inside, subtotal = (start, start)
        for k in reversed(range(size)):
            passed = k > position
            subtotal = combine(subtotal, pieces[k])
            inside = jnp.where(passed, subtotal, inside)
        before = combine(inside, before)
    return before


def collected_together(shard, axis):
    leaves = jax.tree.leaves(shard)
    order = sorted(range(len(leaves)), key=lambda k: -leaves[k].size)
    width = (1, *leaves[order[0]].shape)[-1]
    lines = [
        jnp.pad(leaves[k].reshape(-1), (0, -leaves[k].size % width)).reshape(-1, width)
        for k in order
    ]
    both, at, found = (lax.all_gather(jnp.concatenate(lines), axis), 0, {})
    for k, line in zip(order, lines):
        section = both[:, at : at + len(line)].reshape(len(both), -1)
        found[k] = section[:, : leaves[k].size].reshape(-1, *leaves[k].shape)
        at += len(line)
    numbers = iter(range(len(leaves)))
    return jax.tree.map(lambda _: found[next(numbers)], shard)


def once_a_type(shard, axis):
    leaves, found = (jax.tree.leaves(shard), {})
    for initial, a in enumerate(leaves):
        if initial not in found:
            alike = [k for k, b in enumerate(leaves) if b.dtype == a.dtype]
            got = (
                collected_together([leaves[k] for k in alike], axis)
                if len(alike) > 1
                else [lax.all_gather(a, axis)]
            )
            for k, b in zip(alike, got):
                found[k] = b
    numbers = iter(range(len(leaves)))
    return jax.tree.map(lambda _: found[next(numbers)], shard)


def entering_2(shard, axes, combine, identity):
    before = start = neutral_like(shard, identity)
    subtotal = shard
    for axis in reversed(axes):
        size, position = (lax.axis_size(axis), lax.axis_index(axis))
        pieces = once_a_type(subtotal, axis)
        inside, subtotal = (start, start)
        for k in range(size):
            passed = k < position
            subtotal = combine(subtotal, jax.tree.map(lambda part: part[k], pieces))
            inside = jax.tree.map(lambda new, old: jnp.where(passed, new, old), subtotal, inside)
        before = combine(inside, before)
    return before


def from_everyone(shard, axis):
    size = lax.axis_size(axis)
    return lax.all_to_all(
        jnp.broadcast_to(shard[None], (size, *shard.shape)), axis, 0, 0, tiled=True
    )


def laid_out(blocks, dim):
    blocks = jnp.moveaxis(blocks, 0, dim)
    shape = blocks.shape
    return blocks.reshape(*shape[:dim], shape[dim] * shape[dim + 1], *shape[dim + 2 :])


def gathered_copies(shard, axis, dim):
    blocks = from_everyone(shard, axis)
    return laid_out(blocks, dim)


def taken_together(shard, axis):
    everything = from_everyone(shard, axis)
    return jnp.sum(everything, axis=0)


def cut_along(shard, dim, size):
    before, after = (shard.shape[:dim], shard.shape[dim + 1 :])
    return jnp.moveaxis(shard.reshape(*before, size, -1, *after), dim, 0)


def sum_at_owner(shard, axis, dim):
    size = lax.axis_size(axis)
    blocks = lax.all_to_all(cut_along(shard, dim, size), axis, 0, 0, tiled=True)
    return jnp.sum(blocks, axis=0)


def group_bounds(tie_groups):
    length = tie_groups.shape[0]
    row_index = jnp.arange(length, dtype=jnp.int32)
    change = tie_groups[1:] != tie_groups[:-1]
    begins = jnp.concatenate([jnp.ones((1,), jnp.bool_), change])
    finish = jnp.concatenate([change, jnp.ones((1,), jnp.bool_)])
    first_row = lax.cummax(jnp.where(begins, row_index, 0), axis=0)
    last_row = lax.cummin(jnp.where(finish, row_index, length - 1), axis=0, reverse=True)
    return (first_row, last_row)


def add_values(earlier, later_value):
    return jax.tree.map(jnp.add, earlier, later_value)


def shards(predictor, events, tie_groups, node_ids, bin_index):
    hazard_exp = jnp.exp(predictor)
    suffix = jnp.cumsum(hazard_exp[::-1])[::-1]
    later_sum = entering(suffix[0], ROW_FEAT, add_values, jnp.zeros((), jnp.float32))
    first_row, last_row = group_bounds(tie_groups)
    risk_sum = (suffix + later_sum)[first_row]
    failed = events.astype(jnp.float32)
    weight_one = failed / risk_sum
    weight_two = failed / (risk_sum * risk_sum)
    cum_one = jnp.cumsum(weight_one)
    cum_two = jnp.cumsum(weight_two)
    before_one, before_two = entering_2(
        (cum_one[-1], cum_two[-1]),
        ROW_FEAT,
        add_values,
        (jnp.zeros((), jnp.float32), jnp.zeros((), jnp.float32)),
    )
    hazard_one = (cum_one + before_one)[last_row]
    hazard_two = (cum_two + before_two)[last_row]
    gradient = hazard_exp * hazard_one - failed
    hessian = hazard_exp * hazard_one - hazard_exp * hazard_exp * hazard_two
    stats = jnp.stack([gradient, hessian]).astype(jnp.bfloat16)
    levels = jnp.arange(NODES, dtype=jnp.int32)
    bin_levels = jnp.arange(BINS, dtype=jnp.int32)
    feat_count = bin_index.shape[0]
    feat_block = math.gcd(feat_count, 8)
    portion = gathered_copies(stats, FEAT, 1)
    row_count = portion.shape[1]
    node_mask = (node_ids[None, :] == levels[:, None]).astype(jnp.bfloat16)
    weighted = (node_mask[:, None, :] * portion[None, :, :]).reshape(NODES * 2, row_count)
    grouped = bin_index.reshape(feat_count // feat_block, feat_block, row_count)

    def one_block(columns):
        onehot = (columns[:, :, None] == bin_levels).astype(jnp.bfloat16)
        return jnp.einsum("cl,flb->cfb", weighted, onehot, preferred_element_type=jnp.float32)

    blocks = lax.map(one_block, grouped)
    hist = blocks.transpose(1, 0, 2, 3).reshape(NODES * 2, feat_count, BINS)
    summed = taken_together(jnp.sum(hist, axis=2), ROW)
    totals = summed.reshape(NODES, 2, feat_count, 1)
    left_flat = sum_at_owner(jnp.cumsum(hist, axis=2), ROW, 2)
    left_sums = left_flat.reshape(NODES, 2, feat_count, left_flat.shape[2])
    grad_left = left_sums[:, 0]
    hess_left = left_sums[:, 1]
    grad_all = totals[:, 0]
    hess_all = totals[:, 1]
    split_gain = (
        grad_left * grad_left / (hess_left + 1.0)
        + (grad_all - grad_left) ** 2 / (hess_all - hess_left + 1.0)
        - grad_all * grad_all / (hess_all + 1.0)
    )
    return (gradient, hessian, split_gain)


def solution(mesh):
    finer = Mesh(mesh.devices.reshape(4, 8, 4, 2), ("row_0", "row_1", "feat_0", "feat_1"))
    in_specs = (P(ROW_FEAT), P(ROW_FEAT), P(ROW_FEAT), P(ROW), P(FEAT, ROW))
    out_specs = (P(ROW_FEAT), P(ROW_FEAT), P(None, FEAT, ROW))
    return jax.shard_map(
        shards, mesh=finer, in_specs=in_specs, out_specs=out_specs, check_vma=False
    )
```

profile of v0, /device:TPU:32, one launch (start us, length us, event | category | flops | bytes accessed | tf_op | source)
XLA Modules:
  0.0 295.1 jit_solution(1507804462859085230)
XLA Ops:
  15.2 10.7 %all-reduce.1 = f32[4]{0:T(128)S(1)} all-reduce(f32[4]{0:T(128)S(1)} %dynamic-update-slice.1), channel_id=1, replica_groups=mesh['row_0'=4,'row_1'=8,'feat_0'=4,'feat_1'=2] {'feat_0'}, use_global_device_ids=true, to_apply=%add.1 | all-reduce | flops 4 | bytes 32
  30.2 17.9 %all-reduce.2 = f32[8]{0:T(128)S(1)} all-reduce(f32[8]{0:T(128)S(1)} %dynamic-update-slice.2), channel_id=1, replica_groups=mesh['row_0'=4,'row_1'=8,'feat_0'=4,'feat_1'=2] {'row_1'}, use_global_device_ids=true, to_apply=%add.2 | all-reduce | flops 8 | bytes 64
  54.7 10.5 %all-reduce.3 = f32[4]{0:T(128)S(1)} all-reduce(f32[4]{0:T(128)S(1)} %dynamic-update-slice.3), channel_id=1, replica_groups=mesh['row_0'=4,'row_1'=8,'feat_0'=4,'feat_1'=2] {'row_0'}, use_global_device_ids=true, to_apply=%add.3 | all-reduce | flops 4 | bytes 32
  71.7 3.5 %gather_fusion = f32[512]{0:T(512)S(1)} fusion(f32[512]{0:T(512)S(1)} %broadcast_add_fusion.2, s32[1024]{0:T(1024)S(1)} %pad_clamp_fusion.1), kind=kCustom, calls=%fused_computation | custom fusion | bytes 6144 | tf_op jit(solution)/shard_map/gather | solution.py:139
  86.9 7.7 %all-reduce.5 = f32[8]{0:T(128)S(1)} all-reduce(f32[8]{0:T(128)S(1)} %fusion.16), channel_id=3, replica_groups=mesh['row_0'=4,'row_1'=8,'feat_0'=4,'feat_1'=2] {'feat_0'}, use_global_device_ids=true, to_apply=%add.5 | all-reduce | flops 8 | bytes 64
  101.9 16.4 %all-reduce.6 = f32[16]{0:T(128)S(1)} all-reduce(f32[16]{0:T(128)S(1)} %fusion.17), channel_id=4, replica_groups=mesh['row_0'=4,'row_1'=8,'feat_0'=4,'feat_1'=2] {'row_1'}, use_global_device_ids=true, to_apply=%add.6 | all-reduce | flops 16 | bytes 128
  133.1 7.7 %all-reduce.7 = f32[8]{0:T(128)S(1)} all-reduce(f32[8]{0:T(128)S(1)} %fusion.18), channel_id=5, replica_groups=mesh['row_0'=4,'row_1'=8,'feat_0'=4,'feat_1'=2] {'row_0'}, use_global_device_ids=true, to_apply=%add.7 | all-reduce | flops 8 | bytes 64
  147.8 3.5 %gather_fusion.1 = f32[512]{0:T(512)S(1)} fusion(f32[512]{0:T(512)S(1)} %broadcast_add_fusion.1, s32[1024]{0:T(1024)S(1)} %pad_clamp_fusion), kind=kCustom, calls=%fused_computation.1 | custom fusion | bytes 6144 | tf_op jit(solution)/shard_map/gather | solution.py:151
  151.3 3.5 %gather_fusion.2 = f32[512]{0:T(512)S(1)} fusion(f32[512]{0:T(512)S(1)} %broadcast_add_fusion, s32[1024]{0:T(1024)S(1)} %pad_clamp_fusion), kind=kCustom, calls=%fused_computation.2 | custom fusion | bytes 6144 | tf_op jit(solution)/shard_map/gather | solution.py:152
  159.4 5.3 %all-to-all-done = bf16[8,2,512]{2,1,0:T(2,128)(2,1)S(1)} async-done(((bf16[8,2,512]{2,1,0:T(2,128)(2,1)}), bf16[8,2,512]{2,1,0:T(2,128)(2,1)S(1)}, u32[]{:S(2)}, u32[]{:S(2)}) %all-to-all-start) | async-done | bytes 16416 | tf_op jit(solution)/shard_map/all_to_all | solution.py:87
  164.7 61.0 %while.11 = (s32[]{:T(128)}, f32[8,16,8,256]{3,1,2,0:T(8,128)S(1)}, s32[8,8,4096]{2,1,0:T(8,128)}, bf16[2,4096]{1,0:T(2,128)(2,1)S(1)}, bf16[8,4096]{1,0:T(8,128)(2,1)S(1)}, /*index=5*/s32[]{:T(128)}) while((s32[]{:T(128)}, f32[8,16,8,256]{3,1,2,0:T(8,128)S(1)}, s32[8,8,4096]{2,1,0:T(8,128)}, bf16[2,4096]{1,0:T(2,128)(2,1)S(1)}, ...), condition=%wide.region_11.12_spmd.clone, body=%wide.region_10.11_spmd.clone.sunk | while | flops 276889600 | bytes 1130581 | solution.py:170
  165.8 6.5 %fusion.34 = f32[8,16,8,256]{3,1,2,0:T(8,128)S(1)} fusion(f32[8,16,8,256]{3,1,2,0:T(8,128)S(1)} %get-tuple-element.160, s32[]{:T(128)S(6)} %copy.47, bf16[16,4096,1]{1,0,2:T(8,128)(2,1)S(1)} %reshape.437, s32[8,4096]{1,0:T(8,128)S(1)} %dynamic-slice_bitcast_fusion.2), kind=kOutput, calls=%fused_computation.9.clone.1 | convolution fusion | flops 276824064 | bytes 393220 | tf_op jit(solution)/shard_map/while/body/eval_jaxpr/cl,flb->cfb/dot_general | solution.py:168
  173.4 6.5 %fusion.34 = f32[8,16,8,256]{3,1,2,0:T(8,128)S(1)} fusion(f32[8,16,8,256]{3,1,2,0:T(8,128)S(1)} %get-tuple-element.160, s32[]{:T(128)S(6)} %copy.47, bf16[16,4096,1]{1,0,2:T(8,128)(2,1)S(1)} %reshape.437, s32[8,4096]{1,0:T(8,128)S(1)} %dynamic-slice_bitcast_fusion.2), kind=kOutput, calls=%fused_computation.9.clone.1 | convolution fusion | flops 276824064 | bytes 393220 | tf_op jit(solution)/shard_map/while/body/eval_jaxpr/cl,flb->cfb/dot_general | solution.py:168
  181.1 6.5 %fusion.34 = f32[8,16,8,256]{3,1,2,0:T(8,128)S(1)} fusion(f32[8,16,8,256]{3,1,2,0:T(8,128)S(1)} %get-tuple-element.160, s32[]{:T(128)S(6)} %copy.47, bf16[16,4096,1]{1,0,2:T(8,128)(2,1)S(1)} %reshape.437, s32[8,4096]{1,0:T(8,128)S(1)} %dynamic-slice_bitcast_fusion.2), kind=kOutput, calls=%fused_computation.9.clone.1 | convolution fusion | flops 276824064 | bytes 393220 | tf_op jit(solution)/shard_map/while/body/eval_jaxpr/cl,flb->cfb/dot_general | solution.py:168
  188.7 6.5 %fusion.34 = f32[8,16,8,256]{3,1,2,0:T(8,128)S(1)} fusion(f32[8,16,8,256]{3,1,2,0:T(8,128)S(1)} %get-tuple-element.160, s32[]{:T(128)S(6)} %copy.47, bf16[16,4096,1]{1,0,2:T(8,128)(2,1)S(1)} %reshape.437, s32[8,4096]{1,0:T(8,128)S(1)} %dynamic-slice_bitcast_fusion.2), kind=kOutput, calls=%fused_computation.9.clone.1 | convolution fusion | flops 276824064 | bytes 393220 | tf_op jit(solution)/shard_map/while/body/eval_jaxpr/cl,flb->cfb/dot_general | solution.py:168
  196.3 6.5 %fusion.34 = f32[8,16,8,256]{3,1,2,0:T(8,128)S(1)} fusion(f32[8,16,8,256]{3,1,2,0:T(8,128)S(1)} %get-tuple-element.160, s32[]{:T(128)S(6)} %copy.47, bf16[16,4096,1]{1,0,2:T(8,128)(2,1)S(1)} %reshape.437, s32[8,4096]{1,0:T(8,128)S(1)} %dynamic-slice_bitcast_fusion.2), kind=kOutput, calls=%fused_computation.9.clone.1 | convolution fusion | flops 276824064 | bytes 393220 | tf_op jit(solution)/shard_map/while/body/eval_jaxpr/cl,flb->cfb/dot_general | solution.py:168
  203.9 6.5 %fusion.34 = f32[8,16,8,256]{3,1,2,0:T(8,128)S(1)} fusion(f32[8,16,8,256]{3,1,2,0:T(8,128)S(1)} %get-tuple-element.160, s32[]{:T(128)S(6)} %copy.47, bf16[16,4096,1]{1,0,2:T(8,128)(2,1)S(1)} %reshape.437, s32[8,4096]{1,0:T(8,128)S(1)} %dynamic-slice_bitcast_fusion.2), kind=kOutput, calls=%fused_computation.9.clone.1 | convolution fusion | flops 276824064 | bytes 393220 | tf_op jit(solution)/shard_map/while/body/eval_jaxpr/cl,flb->cfb/dot_general | solution.py:168
  211.6 6.5 %fusion.34 = f32[8,16,8,256]{3,1,2,0:T(8,128)S(1)} fusion(f32[8,16,8,256]{3,1,2,0:T(8,128)S(1)} %get-tuple-element.160, s32[]{:T(128)S(6)} %copy.47, bf16[16,4096,1]{1,0,2:T(8,128)(2,1)S(1)} %reshape.437, s32[8,4096]{1,0:T(8,128)S(1)} %dynamic-slice_bitcast_fusion.2), kind=kOutput, calls=%fused_computation.9.clone.1 | convolution fusion | flops 276824064 | bytes 393220 | tf_op jit(solution)/shard_map/while/body/eval_jaxpr/cl,flb->cfb/dot_general | solution.py:168
  219.2 6.5 %fusion.34 = f32[8,16,8,256]{3,1,2,0:T(8,128)S(1)} fusion(f32[8,16,8,256]{3,1,2,0:T(8,128)S(1)} %get-tuple-element.160, s32[]{:T(128)S(6)} %copy.47, bf16[16,4096,1]{1,0,2:T(8,128)(2,1)S(1)} %reshape.437, s32[8,4096]{1,0:T(8,128)S(1)} %dynamic-slice_bitcast_fusion.2), kind=kOutput, calls=%fused_computation.9.clone.1 | convolution fusion | flops 276824064 | bytes 393220 | tf_op jit(solution)/shard_map/while/body/eval_jaxpr/cl,flb->cfb/dot_general | solution.py:168
  227.1 9.5 %reduce-window.75 = f32[16,64,2,128]{3,1,2,0:T(8,128)S(1)} reduce-window(f32[16,64,2,128]{3,1,2,0:T(8,128)S(1)} %copy.25, f32[]{:T(128)} %constant.23.clone.1), window={size=1x1x1x128 pad=0_0x0_0x0_0x127_0}, to_apply=%region_12.13 | reduce-window | flops 33292288 | bytes 2097156 | tf_op jit(solution)/shard_map/reduce-window.10
  239.5 6.3 %all-to-all-start.2 = ((f32[32,1,1024]{2,1,0:T(1,128)}), f32[32,1,1024]{2,1,0:T(1,128)S(1)}, u32[]{:S(2)}, u32[]{:S(2)}) async-start(f32[32,1,1024]{2,1,0:T(1,128)} %reshape.434), calls=%async_computation.2 | async-start | bytes 262144 | tf_op jit(solution)/shard_map/all_to_all | solution.py:87
  249.1 3.4 %reshape.432 = f32[32,1,8192]{2,1,0:T(1,128)} reshape(f32[32,16,8,64]{3,2,1,0:T(8,128)} %copy_bitcast_fusion) | data formatting | bytes 2097152
  255.5 6.9 %all-to-all-start.1 = ((f32[32,1,8192]{2,1,0:T(1,128)}), f32[32,1,8192]{2,1,0:T(1,128)S(1)}, u32[]{:S(2)}, u32[]{:S(2)}) async-start(f32[32,1,8192]{2,1,0:T(1,128)} %reshape.432), calls=%async_computation.1 | async-start | bytes 2097152 | tf_op jit(solution)/shard_map/all_to_all | solution.py:115
  264.0 26.3 %all-to-all-done.1 = f32[32,1,8192]{2,1,0:T(1,128)S(1)} async-done(((f32[32,1,8192]{2,1,0:T(1,128)}), f32[32,1,8192]{2,1,0:T(1,128)S(1)}, u32[]{:S(2)}, u32[]{:S(2)}) %all-to-all-start.1) | async-done | bytes 1048608 | tf_op jit(solution)/shard_map/all_to_all | solution.py:115
  (136 shorter events, 59.1 us)
Async XLA Ops:
  0.6 74.5 %copy-start.2 = (s32[512]{0:T(512)S(1)}, s32[512]{0:T(512)}, u32[]{:S(2)}) copy-start(s32[512]{0:T(512)} %param.8) | copy-start | bytes 6148
  147.8 7.0 %copy-start.1 = (f32[512]{0:T(512)S(1)}, f32[512]{0:T(512)}, u32[]{:S(2)}) copy-start(f32[512]{0:T(512)} %param.7) | copy-start | bytes 6148
  147.8 11.6 %copy-start = (s32[4096]{0:T(1024)S(1)}, s32[4096]{0:T(1024)}, u32[]{:S(2)}) copy-start(s32[4096]{0:T(1024)} %param.10) | copy-start | bytes 49156
  156.0 8.6 %all-to-all-start = ((bf16[8,2,512]{2,1,0:T(2,128)(2,1)}), bf16[8,2,512]{2,1,0:T(2,128)(2,1)S(1)}, u32[]{:S(2)}, u32[]{:S(2)}) async-start(bf16[8,2,512]{2,1,0:T(2,128)(2,1)} %broadcast_in_dim.42), calls=%async_computation | async-start | bytes 32768 | tf_op jit(solution)/shard_map/all_to_all | solution.py:87
  239.5 16.0 %all-to-all-start.2 = ((f32[32,1,1024]{2,1,0:T(1,128)}), f32[32,1,1024]{2,1,0:T(1,128)S(1)}, u32[]{:S(2)}, u32[]{:S(2)}) async-start(f32[32,1,1024]{2,1,0:T(1,128)} %reshape.434), calls=%async_computation.2 | async-start | bytes 262144 | tf_op jit(solution)/shard_map/all_to_all | solution.py:87
  255.5 34.8 %all-to-all-start.1 = ((f32[32,1,8192]{2,1,0:T(1,128)}), f32[32,1,8192]{2,1,0:T(1,128)S(1)}, u32[]{:S(2)}, u32[]{:S(2)}) async-start(f32[32,1,8192]{2,1,0:T(1,128)} %reshape.432), calls=%async_computation.1 | async-start | bytes 2097152 | tf_op jit(solution)/shard_map/all_to_all | solution.py:115
where the time goes:
time: 297 us; the launch traced here: 295 us
  blocking collectives  75.8 us (26%)
  matrix products  51.8 us (17%)
  local copies, waits for them, and re-layouts  45.9 us (15%)
  between operations  45.1 us (15%)
  waiting for transfers between devices  34.5 us (12%)
  other arithmetic  25.4 us (9%)
  starting transfers between devices  16.5 us (6%)
    unnamed x8, blocking collectives  75.8 us
    dot_general x8, matrix products, one_block(): jnp.einsum('cl,flb->cfb', weighted, onehot, preferred_element_type=jnp.fl...  51.8 us
    all_to_all x1, waiting for transfers between devices, sum_at_owner(): blocks = lax.all_to_all(cut_along(shard, dim, size), axis, 0, 0, tiled=True)  26.3 us
    another operation x17, other arithmetic  14.2 us
    unnamed x26, local copies, waits for them, and re-layouts  13.3 us
    all_to_all x2, starting transfers between devices, from_everyone(): lax.all_to_all(jnp.broadcast_to(shard[None], (size, *shard.shape)), axis,...  9.59 us
    all_to_all x2, waiting for transfers between devices, from_everyone(): lax.all_to_all(jnp.broadcast_to(shard[None], (size, *shard.shape)), axis,...  8.18 us
    eq x8, local copies, waits for them, and re-layouts, one_block(): onehot = (columns[:, :, None] == bin_levels).astype(jnp.bfloat16)  7.35 us
  transfers between devices with their start and end apart: 3, of which 3 were waited for; matrix products, arithmetic and copies ran while one was open for 3% of the time, Pallas kernels for 0%

commit v1 on v0

v1 whole, which is shorter than its diff:
```python
import jax
import jax.numpy as jnp
from jax import lax
from jax.experimental import pallas as pl
from jax.experimental.pallas import tpu as pltpu
from jax.sharding import Mesh
from jax.sharding import PartitionSpec as P

NODES = 8
LANES = 128
FEAT = ("feat_0", "feat_1")
ROW = ("row_0", "row_1")
ROW_FEAT = ROW + FEAT
BF = jnp.bfloat16
F32 = jnp.float32
FAR = 1e30
CHUNK = 512
GROUP = 2


def iota(shape, dim):
    return lax.broadcasted_iota(jnp.int32, shape, dim)


def thirds(x):
    first = x.astype(BF)
    left = x - first.astype(F32)
    second = left.astype(BF)
    third = (left - second.astype(F32)).astype(BF)
    return first, second, third


def times_right(x, ones):
    rows = x.shape[0]
    y = jnp.dot(jnp.concatenate(thirds(x), 0), ones, preferred_element_type=F32)
    return y[:rows] + y[rows : 2 * rows] + y[2 * rows :]


def times_left(ones, x):
    width = x.shape[1]
    y = jnp.dot(ones, jnp.concatenate(thirds(x), 1), preferred_element_type=F32)
    return y[:, :width] + y[:, width : 2 * width] + y[:, 2 * width :]


def as_ones(mask):
    return jnp.where(mask, 1.0, 0.0).astype(BF)


def spread_kernel(pred_ref, ev_ref, tie_ref, out_ref):
    three = jnp.concatenate(
        [pred_ref[...], ev_ref[...].astype(F32), tie_ref[...].astype(F32)], 0
    )
    for k in range(out_ref.shape[0]):
        out_ref[k] = three


def risk_kernel(got_ref, msg_ref, own_ref):
    blocks, quarter = got_ref.shape[0], got_ref.shape[1] // 3
    rows = blocks * quarter
    for k in range(blocks):
        for j in range(3):
            own_ref[j, k * quarter : (k + 1) * quarter, :] = got_ref[
                k, j * quarter : (j + 1) * quarter, :
            ]
    hazard = jnp.exp(own_ref[0])
    tie = own_ref[2]
    own_ref[0] = hazard
    lanes = (LANES, LANES)
    inside = times_right(hazard, as_ones(iota(lanes, 0) >= iota(lanes, 1)))
    totals = jnp.broadcast_to(inside[:, 0:1], inside.shape)
    square = (rows, rows)
    suffix = inside + times_left(as_ones(iota(square, 1) > iota(square, 0)), totals)
    place = iota((rows, LANES), 1) % 8
    first = suffix
    for k in (1, 2, 4):
        same = (pltpu.roll(tie, k, 1) == tie) & (place >= k)
        first = jnp.where(same, pltpu.roll(first, k, 1), first)
    own_ref[3] = first
    value = jnp.where(own_ref[1] > 0.5, first, FAR)
    total = jnp.broadcast_to(suffix[0:1, 0:1], (8, LANES))
    for k in range(msg_ref.shape[0]):
        msg_ref[k, 0:rows, :] = value
        msg_ref[k, rows : rows + 8, :] = total


def hist_kernel(
    got_ref, own_ref, node_ref, hi_ref, lo_ref,
    grad_ref, hess_ref, out_ref, grad_buf, hess_buf, stat_buf,
):
    shards, rows = got_ref.shape[0], own_ref.shape[1]
    row, feat = lax.axis_index(ROW), lax.axis_index(FEAT)
    later = own_later = jnp.zeros((1, LANES), F32)
    sum_one = sum_two = jnp.zeros((rows, LANES), F32)
    for k in reversed(range(shards)):
        value = got_ref[k, 0:rows, :]
        total = got_ref[k, rows : rows + 1, :]
        weight = jnp.where((value < FAR * 0.1) & (k < row), 1.0 / (value + later), 0.0)
        sum_one += weight
        sum_two += weight * weight
        own_later = jnp.where(k > row, own_later + total, own_later)
        later += total

    def whole(x):
        return jnp.sum(jnp.sum(x, 0, keepdims=True), 1, keepdims=True)

    hazard, failed, tie = own_ref[0], own_ref[1], own_ref[2]
    risk = own_ref[3] + own_later
    one = failed / risk
    both = jnp.concatenate([one, failed / (risk * risk)], 0)
    lanes = (LANES, LANES)
    inside = times_right(both, as_ones(iota(lanes, 0) <= iota(lanes, 1)))
    totals = jnp.broadcast_to(inside[:, LANES - 1 : LANES], inside.shape)
    square = (2 * rows, 2 * rows)
    earlier = (iota(square, 1) < iota(square, 0)) & (
        iota(square, 1) // rows == iota(square, 0) // rows
    )
    upto = inside + times_left(as_ones(earlier), totals)
    haz_one = upto[:rows] + whole(sum_one)
    haz_two = upto[rows:] + whole(sum_two)
    place = iota((rows, LANES), 1) % 8
    for k in (1, 2, 4):
        same = (pltpu.roll(tie, LANES - k, 1) == tie) & (place < 8 - k)
        haz_one = jnp.where(same, pltpu.roll(haz_one, LANES - k, 1), haz_one)
        haz_two = jnp.where(same, pltpu.roll(haz_two, LANES - k, 1), haz_two)
    gradient = hazard * haz_one - failed
    hessian = hazard * haz_one - hazard * hazard * haz_two
    grad_buf[...] = gradient
    hess_buf[...] = hessian
    quarter = grad_ref.shape[0]
    grad_ref[...] = grad_buf[pl.ds(feat * quarter, quarter), :]
    hess_ref[...] = hess_buf[pl.ds(feat * quarter, quarter), :]

    levels = iota((NODES, LANES), 0)
    for k in range(rows):
        here = node_ref[k : k + 1, :] == levels
        stat = jnp.concatenate(
            [
                jnp.where(here, gradient[k : k + 1, :], 0.0),
                jnp.where(here, hessian[k : k + 1, :], 0.0),
            ],
            0,
        )
        stat_buf[:, k * LANES : (k + 1) * LANES] = stat.astype(BF)

    feats, length = hi_ref.shape
    tops = iota((shards, CHUNK), 0).astype(F32).astype(BF)
    zero, unit = jnp.zeros((), BF), jnp.ones((), BF)

    def some_features(g, _):
        acc = None
        for c in range(length // CHUNK):
            cols = pl.ds(c * CHUNK, CHUNK)
            stat = stat_buf[:, cols]
            tall, wide = [], []
            for j in range(GROUP):
                at = pl.ds(g * GROUP + j, 1)
                lo = jnp.broadcast_to(lo_ref[at, cols], (2 * NODES, CHUNK)).astype(BF)
                hi = jnp.broadcast_to(hi_ref[at, cols], (2 * NODES, CHUNK)).astype(BF)
                hi = jnp.concatenate([hi, hi], 0)
                tall.append(jnp.where(hi == tops, unit, zero))
                for b in range(7):
                    wide.append(jnp.where(lo <= jnp.asarray(b, BF), stat, zero))
                wide.append(stat)
            part = lax.dot_general(
                jnp.concatenate(tall, 0), jnp.concatenate(wide, 0),
                (((1,), (1,)), ((), ())), preferred_element_type=F32,
            )
            acc = part if acc is None else acc + part
        for j in range(GROUP):
            out_ref[:, g * GROUP + j, :] = acc[
                shards * j : shards * (j + 1), LANES * j : LANES * (j + 1)
            ]
        return 0

    lax.fori_loop(0, feats // GROUP, some_features, 0)

    last = iota((8, LANES), 1) >= LANES - 2 * NODES

    def eight_features(g, _):
        at = pl.ds(pl.multiple_of(g * 8, 8), 8)
        below = jnp.zeros((8, LANES), F32)
        for k in range(shards):
            block = out_ref[k, at, :]
            out_ref[k, at, :] = block + below
            step = jnp.where(last, block, 0.0)
            for shift in (64, 32, 16):
                step += pltpu.roll(step, shift, 1)
            below += step
        return 0

    lax.fori_loop(0, feats // 8, eight_features, 0)
    final = out_ref[shards - 1, 0:8, :]
    for k in range(shards):
        out_ref[k, feats : feats + 8, :] = final


def gain_kernel(got_ref, out_ref):
    shards, feats = got_ref.shape[0], got_ref.shape[1] - 8
    left = got_ref[0]
    for k in range(1, shards):
        left += got_ref[k]
    total = left[feats : feats + 1, :]
    left = left[:feats]
    total = jnp.where(iota((1, LANES), 1) >= LANES - 2 * NODES, total, 0.0)
    for shift in (64, 32, 16):
        total += pltpu.roll(total, shift, 1)
    grad, hess = left, pltpu.roll(left, LANES - NODES, 1)
    grad_all, hess_all = total, pltpu.roll(total, LANES - NODES, 1)
    gain = (
        grad * grad / (hess + 1.0)
        + (grad_all - grad) * (grad_all - grad) / (hess_all - hess + 1.0)
        - grad_all * grad_all / (hess_all + 1.0)
    )
    gain = jnp.where(iota(gain.shape, 1) % (2 * NODES) < NODES, gain, 0.0)
    shape = (NODES * 8, LANES)
    spot, lane = iota(shape, 0), iota(shape, 1)
    chosen = as_ones(lane == (spot % 8) * 2 * NODES + spot // 8)
    turned = None
    for part in thirds(gain):
        one = lax.dot_general(
            chosen, part, (((1,), (1,)), ((), ())), preferred_element_type=F32
        )
        turned = one if turned is None else turned + one
    for n in range(NODES):
        out_ref[n] = turned[n * 8 : (n + 1) * 8, :]


def call(kernel, outs, n_in, name, scratch=()):
    vmem = pl.BlockSpec(memory_space=pltpu.VMEM)
    return pl.pallas_call(
        kernel,
        out_shape=outs,
        in_specs=[vmem] * n_in,
        out_specs=jax.tree.map(lambda _: vmem, outs),
        scratch_shapes=scratch,
        compiler_params=pltpu.CompilerParams(vmem_limit_bytes=48 << 20),
        name=name,
    )


def exchange(blocks, axes):
    return lax.all_to_all(blocks, axes, 0, 0, tiled=True)


def shards(predictor, events, tie_groups, node_ids, bin_index):
    shape = jax.ShapeDtypeStruct
    n_row, n_feat = lax.axis_size(ROW), lax.axis_size(FEAT)
    quarter = predictor.shape[0] // LANES
    rows = quarter * n_feat
    feats, length = bin_index.shape
    lines = [a.reshape(quarter, LANES) for a in (predictor, events, tie_groups)]
    spread = call(spread_kernel, shape((n_feat, 3 * quarter, LANES), F32), 3, "spread")(*lines)
    got = exchange(spread, FEAT)
    message, own = call(
        risk_kernel,
        (shape((n_row, rows + 8, LANES), F32), shape((4, rows, LANES), F32)),
        1,
        "risk",
    )(got)
    received = exchange(message, ROW)
    hi = (bin_index // 8).astype(F32)
    lo = (bin_index % 8).astype(F32)
    gradient, hessian, left = call(
        hist_kernel,
        (
            shape((quarter, LANES), F32),
            shape((quarter, LANES), F32),
            shape((n_row, feats + 8, LANES), F32),
        ),
        5,
        "hist",
        (
            pltpu.VMEM((rows, LANES), F32),
            pltpu.VMEM((rows, LANES), F32),
            pltpu.VMEM((2 * NODES, length), BF),
        ),
    )(received, own, node_ids.reshape(rows, LANES), hi, lo)
    summed = exchange(left, ROW)
    gain = call(gain_kernel, shape((NODES, 8, feats), F32), 1, "gain")(summed)
    return gradient.reshape(-1), hessian.reshape(-1), gain.transpose(0, 2, 1)


def solution(mesh):
    finer = Mesh(mesh.devices.reshape(4, 8, 4, 2), ROW_FEAT)
    in_specs = (P(ROW_FEAT), P(ROW_FEAT), P(ROW_FEAT), P(ROW), P(FEAT, ROW))
    out_specs = (P(ROW_FEAT), P(ROW_FEAT), P(None, FEAT, ROW))
    return jax.shard_map(
        shards, mesh=finer, in_specs=in_specs, out_specs=out_specs, check_vma=False
    )
```

time: 297 us -> 111 us (0.37)
  matrix products: 51.8 us -> 0 us
  between operations: 45.1 us -> 0.66 us
  local copies, waits for them, and re-layouts: 45.9 us -> 2.04 us
  Pallas kernels: 0 us -> 30 us
  blocking collectives: 75.8 us -> 46.2 us
  other arithmetic: 25.4 us -> 2.18 us
  waiting for transfers between devices: 34.5 us -> 18 us
  starting transfers between devices: 16.5 us -> 11.2 us
    unnamed x8 -> x0, blocking collectives: 75.8 us -> none
    dot_general x8 -> x0, matrix products: 51.8 us -> none  [one_block(): jnp.einsum('cl,flb->cfb', weighted, onehot, preferred_element_type=jnp.fl...]
    all_to_all x0 -> x2, blocking collectives: none -> 46.2 us  [exchange(): return lax.all_to_all(blocks, axes, 0, 0, tiled=True)]
    pallas_call x0 -> x4, Pallas kernels: none -> 30 us  [the longest x1 27.5 us: shards(): call(hist_kernel, (shape((quarter, LANES), F32), shape((quarter, LANES),...]
    all_to_all x3 -> x1, waiting for transfers between devices: 34.5 us -> 18 us  [exchange(): return lax.all_to_all(blocks, axes, 0, 0, tiled=True)]
    another operation x20 -> x0, other arithmetic: 14.3 us -> none
    unnamed x26 -> x8, local copies, waits for them, and re-layouts: 13.3 us -> 2.04 us
    gather x3 -> x0, local copies, waits for them, and re-layouts: 10.5 us -> none  [the longest x1 3.49 us: shards(): risk_sum = (suffix + later_sum)[first_row]]
  transfers between devices with their start and end apart: 3 -> 1, of which waited for: 3 -> 1; matrix products, arithmetic and copies ran while one was open for 3% -> 2% of each run, Pallas kernels for 0% -> 0%
where the time goes in v1:
time: 111 us; the launch traced here: 110 us
  blocking collectives  46.2 us (42%)
  Pallas kernels  30 us (27%)
  waiting for transfers between devices  18 us (16%)
  starting transfers between devices  11.2 us (10%)
  other arithmetic  2.18 us (2%)
  local copies, waits for them, and re-layouts  2.04 us (2%)
    all_to_all x2, blocking collectives, exchange(): return lax.all_to_all(blocks, axes, 0, 0, tiled=True)  46.2 us
    pallas_call x1, Pallas kernels, shards(): call(hist_kernel, (shape((quarter, LANES), F32), shape((quarter, LANES),...  27.5 us
    all_to_all x1, waiting for transfers between devices, exchange(): return lax.all_to_all(blocks, axes, 0, 0, tiled=True)  18 us
    all_to_all x1, starting transfers between devices, exchange(): return lax.all_to_all(blocks, axes, 0, 0, tiled=True)  11.2 us
  transfers between devices with their start and end apart: 1, of which 1 were waited for; matrix products, arithmetic and copies ran while one was open for 2% of the time, Pallas kernels for 0%

profile of v1, /device:TPU:32, one launch (start us, length us, event | category | flops | bytes accessed | tf_op | source)
XLA Modules:
  0.0 110.2 jit_solution(13162128103084508866)
XLA Ops:
  0.6 0.0 copy-start.1
  0.6 0.7 copy-done.1
  1.3 0.0 copy-start.2
  1.3 0.7 copy-done.2
  2.0 0.0 copy-start.3
  2.0 0.7 copy-done.3
  2.7 9.9 %all_to_all.15.got_ref = f32[8,12,128]{2,1,0:T(8,128)S(1)} all-to-all(f32[8,12,128]{2,1,0:T(8,128)S(1)} %spread.1), channel_id=1, replica_groups=mesh['row_0'=4,'row_1'=8,'feat_0'=4,'feat_1'=2] {'feat_0','feat_1'}, dimensions={0} | all-to-all | bytes 98304 | tf_op jit(solution)/shard_map/all_to_all | solution.py:242
  12.6 1.4 %risk.1 = (f32[32,40,128]{2,1,0:T(8,128)}, f32[4,32,128]{2,1,0:T(8,128)S(1)}) custom-call(f32[8,12,128]{2,1,0:T(8,128)S(1)} %all_to_all.15.got_ref), custom_call_target="tpu_custom_call" | custom-call | tf_op jit(solution)/shard_map/risk/pallas_call | solution.py:254
  14.0 11.2 %all-to-all-start.1 = ((f32[32,40,128]{2,1,0:T(8,128)}), f32[32,40,128]{2,1,0:T(8,128)S(1)}, u32[]{:S(2)}, u32[]{:S(2)}) async-start(f32[32,40,128]{2,1,0:T(8,128)} %get-tuple-element.8), calls=%async_computation.1 | async-start | bytes 1310720 | tf_op jit(solution)/shard_map/all_to_all | solution.py:242
  25.2 0.0 copy-start
  25.2 2.2 %fusion.1 = (f32[64,4096]{1,0:T(8,128)S(1)}, f32[64,4096]{1,0:T(8,128)S(1)}) fusion(s32[64,4096]{1,0:T(8,128)} %param.9), kind=kLoop, calls=%fused_computation.6 | loop fusion | flops 5505024 | bytes 3145728 | tf_op jit(solution)/shard_map/convert_element_type | solution.py:262
  27.4 18.0 %all-to-all-done.1.got_ref = f32[32,40,128]{2,1,0:T(8,128)S(1)} async-done(((f32[32,40,128]{2,1,0:T(8,128)}), f32[32,40,128]{2,1,0:T(8,128)S(1)}, u32[]{:S(2)}, u32[]{:S(2)}) %all-to-all-start.1) | async-done | bytes 655392 | tf_op jit(solution)/shard_map/all_to_all | solution.py:242
  45.4 0.0 copy-done
  45.4 27.5 %hist.1 = (f32[4,128]{1,0:T(4,128)}, f32[4,128]{1,0:T(4,128)}, f32[32,72,128]{2,1,0:T(8,128)S(1)}) custom-call(f32[32,40,128]{2,1,0:T(8,128)S(1)} %all-to-all-done.1.got_ref, f32[4,32,128]{2,1,0:T(8,128)S(1)} %get-tuple-element.9.own_ref, s32[32,128]{1,0:T(8,128)S(1)} %bitcast.7, f32[64,4096]{1,0:T(8,128)S(1)} %get-tuple-element.14.hi_ref, ...), custom_call_target="tpu_custom_call" | custom-call | tf_op jit(solution)/shard_map/hist/pallas_call | solution.py:263
  72.8 36.3 %all_to_all.16.got_ref = f32[32,72,128]{2,1,0:T(8,128)S(1)} all-to-all(f32[32,72,128]{2,1,0:T(8,128)S(1)} %get-tuple-element.12), channel_id=1, replica_groups=mesh['row_0'=4,'row_1'=8,'feat_0'=4,'feat_1'=2] {'row_0','row_1'}, dimensions={0} | all-to-all | bytes 2359296 | tf_op jit(solution)/shard_map/all_to_all | solution.py:242
  109.1 1.1 gain.1
  (1 shorter events, 0.0 us)
Async XLA Ops:
  0.6 0.7 copy-start.1
  1.3 0.7 copy-start.2
  2.0 0.7 copy-start.3
  14.0 31.4 %all-to-all-start.1 = ((f32[32,40,128]{2,1,0:T(8,128)}), f32[32,40,128]{2,1,0:T(8,128)S(1)}, u32[]{:S(2)}, u32[]{:S(2)}) async-start(f32[32,40,128]{2,1,0:T(8,128)} %get-tuple-element.8), calls=%async_computation.1 | async-start | bytes 1310720 | tf_op jit(solution)/shard_map/all_to_all | solution.py:242
  25.2 20.2 %copy-start = (s32[4096]{0:T(1024)S(1)}, s32[4096]{0:T(1024)}, u32[]{:S(2)}) copy-start(s32[4096]{0:T(1024)} %param.8) | copy-start | bytes 49156

commit v2 on v1

--- a/solution.py
+++ b/solution.py
@@ -13,9 +13,9 @@
 ROW_FEAT = ROW + FEAT
 BF = jnp.bfloat16
 F32 = jnp.float32
-FAR = 1e30
 CHUNK = 512
 GROUP = 2
+UNROLL = 4
 
 
 def iota(shape, dim):
@@ -46,9 +46,19 @@
     return jnp.where(mask, 1.0, 0.0).astype(BF)
 
 
-def spread_kernel(pred_ref, ev_ref, tie_ref, out_ref):
+def spread_kernel(pred_ref, ev_ref, tie_ref, out_ref, pred, ev, tie, sems):
+    copies = [
+        pltpu.make_async_copy(source, target, sems.at[k])
+        for k, (source, target) in enumerate(
+            ((pred_ref, pred), (ev_ref, ev), (tie_ref, tie))
+        )
+    ]
+    for copy in copies:
+        copy.start()
+    for copy in copies:
+        copy.wait()
     three = jnp.concatenate(
-        [pred_ref[...], ev_ref[...].astype(F32), tie_ref[...].astype(F32)], 0
+        [pred[...], ev[...].astype(F32), tie[...].astype(F32)], 0
     )
     for k in range(out_ref.shape[0]):
         out_ref[k] = three
@@ -76,25 +86,23 @@
         same = (pltpu.roll(tie, k, 1) == tie) & (place >= k)
         first = jnp.where(same, pltpu.roll(first, k, 1), first)
     own_ref[3] = first
-    value = jnp.where(own_ref[1] > 0.5, first, FAR)
-    total = jnp.broadcast_to(suffix[0:1, 0:1], (8, LANES))
+    signed = jnp.where(own_ref[1] > 0.5, first, -first)
     for k in range(msg_ref.shape[0]):
-        msg_ref[k, 0:rows, :] = value
-        msg_ref[k, rows : rows + 8, :] = total
+        msg_ref[k] = signed
 
 
 def hist_kernel(
     got_ref, own_ref, node_ref, hi_ref, lo_ref,
-    grad_ref, hess_ref, out_ref, grad_buf, hess_buf, stat_buf,
+    grad_ref, hess_ref, out_ref, grad_buf, hess_buf, stat_buf, node_buf,
 ):
     shards, rows = got_ref.shape[0], own_ref.shape[1]
     row, feat = lax.axis_index(ROW), lax.axis_index(FEAT)
     later = own_later = jnp.zeros((1, LANES), F32)
     sum_one = sum_two = jnp.zeros((rows, LANES), F32)
     for k in reversed(range(shards)):
-        value = got_ref[k, 0:rows, :]
-        total = got_ref[k, rows : rows + 1, :]
-        weight = jnp.where((value < FAR * 0.1) & (k < row), 1.0 / (value + later), 0.0)
+        value = got_ref[k]
+        total = jnp.broadcast_to(jnp.abs(value[0:1, 0:1]), (1, LANES))
+        weight = jnp.where((value > 0.0) & (k < row), 1.0 / (value + later), 0.0)
         sum_one += weight
         sum_two += weight * weight
         own_later = jnp.where(k > row, own_later + total, own_later)
@@ -130,51 +138,56 @@
     grad_ref[...] = grad_buf[pl.ds(feat * quarter, quarter), :]
     hess_ref[...] = hess_buf[pl.ds(feat * quarter, quarter), :]
 
-    levels = iota((NODES, LANES), 0)
+    wide = (2 * NODES, LANES)
+    levels = iota(wide, 0) % NODES
     for k in range(rows):
-        here = node_ref[k : k + 1, :] == levels
-        stat = jnp.concatenate(
-            [
-                jnp.where(here, gradient[k : k + 1, :], 0.0),
-                jnp.where(here, hessian[k : k + 1, :], 0.0),
-            ],
-            0,
-        )
-        stat_buf[:, k * LANES : (k + 1) * LANES] = stat.astype(BF)
+        cols = slice(k * LANES, (k + 1) * LANES)
+        node_buf[:, cols] = as_ones(node_ref[k : k + 1, :] == levels)
+        for j, stat in enumerate((gradient, hessian)):
+            stat_buf[j, :, cols] = jnp.broadcast_to(stat[k : k + 1, :], wide).astype(BF)
 
     feats, length = hi_ref.shape
     tops = iota((shards, CHUNK), 0).astype(F32).astype(BF)
-    zero, unit = jnp.zeros((), BF), jnp.ones((), BF)
+    bins = (iota((8 * NODES, CHUNK), 0) // NODES).astype(F32).astype(BF)
+    zero = jnp.zeros((), BF)
+    half = iota((shards, LANES), 1) < LANES // 2
 
     def some_features(g, _):
         acc = None
         for c in range(length // CHUNK):
             cols = pl.ds(c * CHUNK, CHUNK)
-            stat = stat_buf[:, cols]
-            tall, wide = [], []
+            node = jnp.concatenate([node_buf[:, cols]] * 4, 0)
+            grad = jnp.concatenate([stat_buf[0, :, cols]] * 2, 0)
+            hess = jnp.concatenate([stat_buf[1, :, cols]] * 2, 0)
+            upper, lower = [], []
             for j in range(GROUP):
                 at = pl.ds(g * GROUP + j, 1)
                 lo = jnp.broadcast_to(lo_ref[at, cols], (2 * NODES, CHUNK)).astype(BF)
                 hi = jnp.broadcast_to(hi_ref[at, cols], (2 * NODES, CHUNK)).astype(BF)
-                hi = jnp.concatenate([hi, hi], 0)
-                tall.append(jnp.where(hi == tops, unit, zero))
-                for b in range(7):
-                    wide.append(jnp.where(lo <= jnp.asarray(b, BF), stat, zero))
-                wide.append(stat)
+                top = jnp.concatenate([hi] * 2, 0) == tops
+                upper += [jnp.where(top, grad, zero), jnp.where(top, hess, zero)]
+                reached = jnp.concatenate([lo] * 4, 0) <= bins
+                lower.append(jnp.where(reached, node, zero))
             part = lax.dot_general(
-                jnp.concatenate(tall, 0), jnp.concatenate(wide, 0),
+                jnp.concatenate(upper, 0), jnp.concatenate(lower, 0),
                 (((1,), (1,)), ((), ())), preferred_element_type=F32,
             )
             acc = part if acc is None else acc + part
         for j in range(GROUP):
-            out_ref[:, g * GROUP + j, :] = acc[
-                shards * j : shards * (j + 1), LANES * j : LANES * (j + 1)
-            ]
+            rows_of = slice(2 * shards * j, 2 * shards * (j + 1))
+            lanes_of = slice(LANES * (j // 2), LANES * (j // 2 + 1))
+            both = acc[rows_of, lanes_of]
+            grad, hess = both[:shards], both[shards:]
+            if j % 2 == 0:
+                hess = pltpu.roll(hess, LANES // 2, 1)
+            else:
+                grad = pltpu.roll(grad, LANES // 2, 1)
+            out_ref[:, g * GROUP + j, :] = jnp.where(half, grad, hess)
         return 0
 
-    lax.fori_loop(0, feats // GROUP, some_features, 0)
-
-    last = iota((8, LANES), 1) >= LANES - 2 * NODES
+    lax.fori_loop(0, feats // GROUP, some_features, 0, unroll=UNROLL)
+
+    last = iota((8, LANES), 1) % (LANES // 2) >= LANES // 2 - NODES
 
     def eight_features(g, _):
         at = pl.ds(pl.multiple_of(g * 8, 8), 8)
@@ -183,8 +196,8 @@
             block = out_ref[k, at, :]
             out_ref[k, at, :] = block + below
             step = jnp.where(last, block, 0.0)
-            for shift in (64, 32, 16):
-                step += pltpu.roll(step, shift, 1)
+            for shift in (32, 16, 8):
+                step += pltpu.roll(step, LANES - shift, 1)
             below += step
         return 0
 
@@ -201,20 +214,21 @@
         left += got_ref[k]
     total = left[feats : feats + 1, :]
     left = left[:feats]
-    total = jnp.where(iota((1, LANES), 1) >= LANES - 2 * NODES, total, 0.0)
-    for shift in (64, 32, 16):
-        total += pltpu.roll(total, shift, 1)
-    grad, hess = left, pltpu.roll(left, LANES - NODES, 1)
-    grad_all, hess_all = total, pltpu.roll(total, LANES - NODES, 1)
+    last = iota((1, LANES), 1) % (LANES // 2) >= LANES // 2 - NODES
+    total = jnp.where(last, total, 0.0)
+    for shift in (32, 16, 8):
+        total += pltpu.roll(total, LANES - shift, 1)
+    grad, hess = left, pltpu.roll(left, LANES // 2, 1)
+    grad_all, hess_all = total, pltpu.roll(total, LANES // 2, 1)
     gain = (
         grad * grad / (hess + 1.0)
         + (grad_all - grad) * (grad_all - grad) / (hess_all - hess + 1.0)
         - grad_all * grad_all / (hess_all + 1.0)
     )
-    gain = jnp.where(iota(gain.shape, 1) % (2 * NODES) < NODES, gain, 0.0)
+    gain = jnp.where(iota(gain.shape, 1) < LANES // 2, gain, 0.0)
     shape = (NODES * 8, LANES)
     spot, lane = iota(shape, 0), iota(shape, 1)
-    chosen = as_ones(lane == (spot % 8) * 2 * NODES + spot // 8)
+    chosen = as_ones(lane == (spot % 8) * NODES + spot // 8)
     turned = None
     for part in thirds(gain):
         one = lax.dot_general(
@@ -225,12 +239,12 @@
         out_ref[n] = turned[n * 8 : (n + 1) * 8, :]
 
 
-def call(kernel, outs, n_in, name, scratch=()):
+def call(kernel, outs, n_in, name, scratch=(), space=pltpu.VMEM):
     vmem = pl.BlockSpec(memory_space=pltpu.VMEM)
     return pl.pallas_call(
         kernel,
         out_shape=outs,
-        in_specs=[vmem] * n_in,
+        in_specs=[pl.BlockSpec(memory_space=space)] * n_in,
         out_specs=jax.tree.map(lambda _: vmem, outs),
         scratch_shapes=scratch,
         compiler_params=pltpu.CompilerParams(vmem_limit_bytes=48 << 20),
@@ -249,11 +263,18 @@
     rows = quarter * n_feat
     feats, length = bin_index.shape
     lines = [a.reshape(quarter, LANES) for a in (predictor, events, tie_groups)]
-    spread = call(spread_kernel, shape((n_feat, 3 * quarter, LANES), F32), 3, "spread")(*lines)
+    spread = call(
+        spread_kernel,
+        shape((n_feat, 3 * quarter, LANES), F32),
+        3,
+        "spread",
+        [pltpu.VMEM(a.shape, a.dtype) for a in lines] + [pltpu.SemaphoreType.DMA((3,))],
+        pltpu.HBM,
+    )(*lines)
     got = exchange(spread, FEAT)
     message, own = call(
         risk_kernel,
-        (shape((n_row, rows + 8, LANES), F32), shape((4, rows, LANES), F32)),
+        (shape((n_row, rows, LANES), F32), shape((4, rows, LANES), F32)),
         1,
         "risk",
     )(got)
@@ -272,6 +293,7 @@
         (
             pltpu.VMEM((rows, LANES), F32),
             pltpu.VMEM((rows, LANES), F32),
+            pltpu.VMEM((2, 2 * NODES, length), BF),
             pltpu.VMEM((2 * NODES, length), BF),
         ),
     )(received, own, node_ids.reshape(rows, LANES), hi, lo)

time: 111 us -> 94.2 us (0.85)
  Pallas kernels: 30 us -> 16.5 us
  waiting for transfers between devices: 18 us -> 15.3 us
    pallas_call x1, Pallas kernels: 27.5 us -> 13.9 us  [shards(): call(hist_kernel, (shape((quarter, LANES), F32), shape((quarter, LANES),...]
    all_to_all x1, waiting for transfers between devices: 18 us -> 15.3 us  [exchange(): return lax.all_to_all(blocks, axes, 0, 0, tiled=True)]
where the time goes in v2:
time: 94.2 us; the launch traced here: 93.9 us
  blocking collectives  46 us (49%)
  Pallas kernels  16.5 us (18%)
  waiting for transfers between devices  15.3 us (16%)
  starting transfers between devices  11.2 us (12%)
  other arithmetic  2.18 us (2%)
  local copies, waits for them, and re-layouts  2.04 us (2%)
    all_to_all x2, blocking collectives, exchange(): return lax.all_to_all(blocks, axes, 0, 0, tiled=True)  46 us
    all_to_all x1, waiting for transfers between devices, exchange(): return lax.all_to_all(blocks, axes, 0, 0, tiled=True)  15.3 us
    pallas_call x1, Pallas kernels, shards(): call(hist_kernel, (shape((quarter, LANES), F32), shape((quarter, LANES),...  13.9 us
    all_to_all x1, starting transfers between devices, exchange(): return lax.all_to_all(blocks, axes, 0, 0, tiled=True)  11.2 us
    convert_element_type x1, other arithmetic, shards(): lo = (bin_index % 8).astype(F32)  2.18 us
    unnamed x8, local copies, waits for them, and re-layouts  2.04 us
  transfers between devices with their start and end apart: 1, of which 1 were waited for; matrix products, arithmetic and copies ran while one was open for 2% of the time, Pallas kernels for 0%

profile of v2, /device:TPU:32, one launch (start us, length us, event | category | flops | bytes accessed | tf_op | source)
XLA Modules:
  0.0 93.9 jit_solution(15004379473307127076)
XLA Ops:
  0.6 0.0 copy-start.1
  0.6 0.7 copy-done.1
  1.3 0.0 copy-start.2
  1.3 0.7 copy-done.2
  2.0 0.0 copy-start.3
  2.0 0.7 copy-done.3
  2.7 9.9 %all_to_all.15.got_ref = f32[8,12,128]{2,1,0:T(8,128)S(1)} all-to-all(f32[8,12,128]{2,1,0:T(8,128)S(1)} %spread.1), channel_id=1, replica_groups=mesh['row_0'=4,'row_1'=8,'feat_0'=4,'feat_1'=2] {'feat_0','feat_1'}, dimensions={0} | all-to-all | bytes 98304 | tf_op jit(solution)/shard_map/all_to_all | solution.py:256
  12.6 1.4 %risk.1 = (f32[32,32,128]{2,1,0:T(8,128)}, f32[4,32,128]{2,1,0:T(8,128)S(1)}) custom-call(f32[8,12,128]{2,1,0:T(8,128)S(1)} %all_to_all.15.got_ref), custom_call_target="tpu_custom_call" | custom-call | tf_op jit(solution)/shard_map/risk/pallas_call | solution.py:275
  14.0 11.2 %all-to-all-start.1 = ((f32[32,32,128]{2,1,0:T(8,128)}), f32[32,32,128]{2,1,0:T(8,128)S(1)}, u32[]{:S(2)}, u32[]{:S(2)}) async-start(f32[32,32,128]{2,1,0:T(8,128)} %get-tuple-element.8), calls=%async_computation.1 | async-start | bytes 1048576 | tf_op jit(solution)/shard_map/all_to_all | solution.py:256
  25.2 0.0 copy-start
  25.3 2.2 %fusion.1 = (f32[64,4096]{1,0:T(8,128)S(1)}, f32[64,4096]{1,0:T(8,128)S(1)}) fusion(s32[64,4096]{1,0:T(8,128)} %param.9), kind=kLoop, calls=%fused_computation.6 | loop fusion | flops 5505024 | bytes 3145728 | tf_op jit(solution)/shard_map/convert_element_type | solution.py:283
  27.4 15.3 %all-to-all-done.1.got_ref = f32[32,32,128]{2,1,0:T(8,128)S(1)} async-done(((f32[32,32,128]{2,1,0:T(8,128)}), f32[32,32,128]{2,1,0:T(8,128)S(1)}, u32[]{:S(2)}, u32[]{:S(2)}) %all-to-all-start.1) | async-done | bytes 524320 | tf_op jit(solution)/shard_map/all_to_all | solution.py:256
  42.8 0.0 copy-done
  42.8 13.9 %hist.1 = (f32[4,128]{1,0:T(4,128)}, f32[4,128]{1,0:T(4,128)}, f32[32,72,128]{2,1,0:T(8,128)S(1)}) custom-call(f32[32,32,128]{2,1,0:T(8,128)S(1)} %all-to-all-done.1.got_ref, f32[4,32,128]{2,1,0:T(8,128)S(1)} %get-tuple-element.9.own_ref, s32[32,128]{1,0:T(8,128)S(1)} %bitcast.7, f32[64,4096]{1,0:T(8,128)S(1)} %get-tuple-element.14.hi_ref, ...), custom_call_target="tpu_custom_call" | custom-call | tf_op jit(solution)/shard_map/hist/pallas_call | solution.py:284
  56.7 36.1 %all_to_all.16.got_ref = f32[32,72,128]{2,1,0:T(8,128)S(1)} all-to-all(f32[32,72,128]{2,1,0:T(8,128)S(1)} %get-tuple-element.12), channel_id=1, replica_groups=mesh['row_0'=4,'row_1'=8,'feat_0'=4,'feat_1'=2] {'row_0','row_1'}, dimensions={0} | all-to-all | bytes 2359296 | tf_op jit(solution)/shard_map/all_to_all | solution.py:256
  92.8 1.1 %gain.1 = f32[8,8,64]{2,1,0:T(8,128)} custom-call(f32[32,72,128]{2,1,0:T(8,128)S(1)} %all_to_all.16.got_ref), custom_call_target="tpu_custom_call" | custom-call | tf_op jit(solution)/shard_map/gain/pallas_call | solution.py:301
  (1 shorter events, 0.0 us)
Async XLA Ops:
  0.6 0.7 copy-start.1
  1.3 0.7 copy-start.2
  2.0 0.7 copy-start.3
  14.0 28.7 %all-to-all-start.1 = ((f32[32,32,128]{2,1,0:T(8,128)}), f32[32,32,128]{2,1,0:T(8,128)S(1)}, u32[]{:S(2)}, u32[]{:S(2)}) async-start(f32[32,32,128]{2,1,0:T(8,128)} %get-tuple-element.8), calls=%async_computation.1 | async-start | bytes 1048576 | tf_op jit(solution)/shard_map/all_to_all | solution.py:256
  25.2 17.5 %copy-start = (s32[4096]{0:T(1024)S(1)}, s32[4096]{0:T(1024)}, u32[]{:S(2)}) copy-start(s32[4096]{0:T(1024)} %param.8) | copy-start | bytes 49156

commit v3 on v2

--- a/solution.py
+++ b/solution.py
@@ -93,7 +93,7 @@
 
 def hist_kernel(
     got_ref, own_ref, node_ref, hi_ref, lo_ref,
-    grad_ref, hess_ref, out_ref, grad_buf, hess_buf, stat_buf, node_buf,
+    grad_ref, hess_ref, out_ref, grad_buf, hess_buf, stat_buf, node_buf, sums_buf,
 ):
     shards, rows = got_ref.shape[0], own_ref.shape[1]
     row, feat = lax.axis_index(ROW), lax.axis_index(FEAT)
@@ -182,10 +182,8 @@
                 hess = pltpu.roll(hess, LANES // 2, 1)
             else:
                 grad = pltpu.roll(grad, LANES // 2, 1)
-            out_ref[:, g * GROUP + j, :] = jnp.where(half, grad, hess)
+            sums_buf[:, g * GROUP + j, :] = jnp.where(half, grad, hess)
         return 0
-
-    lax.fori_loop(0, feats // GROUP, some_features, 0, unroll=UNROLL)
 
     last = iota((8, LANES), 1) % (LANES // 2) >= LANES // 2 - NODES
 
@@ -193,7 +191,7 @@
         at = pl.ds(pl.multiple_of(g * 8, 8), 8)
         below = jnp.zeros((8, LANES), F32)
         for k in range(shards):
-            block = out_ref[k, at, :]
+            block = sums_buf[k, at, :]
             out_ref[k, at, :] = block + below
             step = jnp.where(last, block, 0.0)
             for shift in (32, 16, 8):
@@ -201,7 +199,13 @@
             below += step
         return 0
 
-    lax.fori_loop(0, feats // 8, eight_features, 0)
+    def both_stages(g, _):
+        for j in range(8 // GROUP):
+            some_features(g * (8 // GROUP) + j, 0)
+        return eight_features(jnp.maximum(g - 1, 0), 0)
+
+    lax.fori_loop(0, feats // 8, both_stages, 0, unroll=UNROLL)
+    eight_features(feats // 8 - 1, 0)
     final = out_ref[shards - 1, 0:8, :]
     for k in range(shards):
         out_ref[k, feats : feats + 8, :] = final
@@ -239,7 +243,7 @@
         out_ref[n] = turned[n * 8 : (n + 1) * 8, :]
 
 
-def call(kernel, outs, n_in, name, scratch=(), space=pltpu.VMEM):
+def call(kernel, outs, n_in, name, scratch=(), space=pltpu.VMEM, limit=48 << 20):
     vmem = pl.BlockSpec(memory_space=pltpu.VMEM)
     return pl.pallas_call(
         kernel,
@@ -247,7 +251,7 @@
         in_specs=[pl.BlockSpec(memory_space=space)] * n_in,
         out_specs=jax.tree.map(lambda _: vmem, outs),
         scratch_shapes=scratch,
-        compiler_params=pltpu.CompilerParams(vmem_limit_bytes=48 << 20),
+        compiler_params=pltpu.CompilerParams(vmem_limit_bytes=limit),
         name=name,
     )
 
@@ -269,7 +273,8 @@
         3,
         "spread",
         [pltpu.VMEM(a.shape, a.dtype) for a in lines] + [pltpu.SemaphoreType.DMA((3,))],
-        pltpu.HBM,
+        pl.ANY,
+        67_000_000,
     )(*lines)
     got = exchange(spread, FEAT)
     message, own = call(
@@ -295,6 +300,7 @@
             pltpu.VMEM((rows, LANES), F32),
             pltpu.VMEM((2, 2 * NODES, length), BF),
             pltpu.VMEM((2 * NODES, length), BF),
+            pltpu.VMEM((n_row, feats, LANES), F32),
         ),
     )(received, own, node_ids.reshape(rows, LANES), hi, lo)
     summed = exchange(left, ROW)

time: 94.2 us -> 91.4 us (0.970)
  local copies, waits for them, and re-layouts: 2.04 us -> 0.01 us
  Pallas kernels: 16.5 us -> 15.4 us
    pallas_call x1, Pallas kernels: 13.9 us -> 11.5 us  [shards(): call(hist_kernel, (shape((quarter, LANES), F32), shape((quarter, LANES),...]
    unnamed x8 -> x2, local copies, waits for them, and re-layouts: 2.04 us -> 0.01 us
    pallas_call x1, Pallas kernels: 0.04 us -> 1.36 us  [shards(): call(spread_kernel, shape((n_feat, 3 * quarter, LANES), F32), 3, 'spread'...]
where the time goes in v3:
time: 91.4 us; the launch traced here: 91 us
  blocking collectives  46.2 us (51%)
  Pallas kernels  15.4 us (17%)
  waiting for transfers between devices  15.3 us (17%)
  starting transfers between devices  11.2 us (12%)
  other arithmetic  2.18 us (2%)
    all_to_all x2, blocking collectives, exchange(): return lax.all_to_all(blocks, axes, 0, 0, tiled=True)  46.2 us
    all_to_all x1, waiting for transfers between devices, exchange(): return lax.all_to_all(blocks, axes, 0, 0, tiled=True)  15.3 us
    pallas_call x1, Pallas kernels, shards(): call(hist_kernel, (shape((quarter, LANES), F32), shape((quarter, LANES),...  11.5 us
    all_to_all x1, starting transfers between devices, exchange(): return lax.all_to_all(blocks, axes, 0, 0, tiled=True)  11.2 us
    convert_element_type x1, other arithmetic, shards(): lo = (bin_index % 8).astype(F32)  2.18 us
  transfers between devices with their start and end apart: 1, of which 1 were waited for; matrix products, arithmetic and copies ran while one was open for 2% of the time, Pallas kernels for 0%

profile of v3, /device:TPU:32, one launch (start us, length us, event | category | flops | bytes accessed | tf_op | source)
XLA Modules:
  0.0 91.0 jit_solution(6932183560808064050)
XLA Ops:
  0.6 1.4 %spread.1 = f32[8,12,128]{2,1,0:T(8,128)} custom-call(f32[4,128]{1,0:T(4,128)} %bitcast.9, s32[4,128]{1,0:T(4,128)} %bitcast.10, s32[4,128]{1,0:T(4,128)} %bitcast.11), custom_call_target="tpu_custom_call" | custom-call | tf_op jit(solution)/shard_map/spread/pallas_call | solution.py:270
  2.0 10.1 %all_to_all.15.got_ref = f32[8,12,128]{2,1,0:T(8,128)S(1)} all-to-all(f32[8,12,128]{2,1,0:T(8,128)} %spread.1), channel_id=1, replica_groups=mesh['row_0'=4,'row_1'=8,'feat_0'=4,'feat_1'=2] {'feat_0','feat_1'}, dimensions={0} | all-to-all | bytes 98304 | tf_op jit(solution)/shard_map/all_to_all | solution.py:260
  12.1 1.4 %risk.1 = (f32[32,32,128]{2,1,0:T(8,128)}, f32[4,32,128]{2,1,0:T(8,128)S(1)}) custom-call(f32[8,12,128]{2,1,0:T(8,128)S(1)} %all_to_all.15.got_ref), custom_call_target="tpu_custom_call" | custom-call | tf_op jit(solution)/shard_map/risk/pallas_call | solution.py:280
  13.5 11.2 %all-to-all-start.1 = ((f32[32,32,128]{2,1,0:T(8,128)}), f32[32,32,128]{2,1,0:T(8,128)S(1)}, u32[]{:S(2)}, u32[]{:S(2)}) async-start(f32[32,32,128]{2,1,0:T(8,128)} %get-tuple-element.8), calls=%async_computation.1 | async-start | bytes 1048576 | tf_op jit(solution)/shard_map/all_to_all | solution.py:260
  24.7 0.0 copy-start
  24.7 2.2 %fusion.1 = (f32[64,4096]{1,0:T(8,128)S(1)}, f32[64,4096]{1,0:T(8,128)S(1)}) fusion(s32[64,4096]{1,0:T(8,128)} %param.9), kind=kLoop, calls=%fused_computation.6 | loop fusion | flops 5505024 | bytes 3145728 | tf_op jit(solution)/shard_map/convert_element_type | solution.py:288
  26.9 15.3 %all-to-all-done.1.got_ref = f32[32,32,128]{2,1,0:T(8,128)S(1)} async-done(((f32[32,32,128]{2,1,0:T(8,128)}), f32[32,32,128]{2,1,0:T(8,128)S(1)}, u32[]{:S(2)}, u32[]{:S(2)}) %all-to-all-start.1) | async-done | bytes 524320 | tf_op jit(solution)/shard_map/all_to_all | solution.py:260
  42.2 0.0 copy-done
  42.2 11.5 %hist.1 = (f32[4,128]{1,0:T(4,128)}, f32[4,128]{1,0:T(4,128)}, f32[32,72,128]{2,1,0:T(8,128)S(1)}) custom-call(f32[32,32,128]{2,1,0:T(8,128)S(1)} %all-to-all-done.1.got_ref, f32[4,32,128]{2,1,0:T(8,128)S(1)} %get-tuple-element.9.own_ref, s32[32,128]{1,0:T(8,128)S(1)} %bitcast.7, f32[64,4096]{1,0:T(8,128)S(1)} %get-tuple-element.14.hi_ref, ...), custom_call_target="tpu_custom_call" | custom-call | tf_op jit(solution)/shard_map/hist/pallas_call | solution.py:289
  53.8 36.1 %all_to_all.16.got_ref = f32[32,72,128]{2,1,0:T(8,128)S(1)} all-to-all(f32[32,72,128]{2,1,0:T(8,128)S(1)} %get-tuple-element.12), channel_id=1, replica_groups=mesh['row_0'=4,'row_1'=8,'feat_0'=4,'feat_1'=2] {'row_0','row_1'}, dimensions={0} | all-to-all | bytes 2359296 | tf_op jit(solution)/shard_map/all_to_all | solution.py:260
  89.9 1.1 %gain.1 = f32[8,8,64]{2,1,0:T(8,128)} custom-call(f32[32,72,128]{2,1,0:T(8,128)S(1)} %all_to_all.16.got_ref), custom_call_target="tpu_custom_call" | custom-call | tf_op jit(solution)/shard_map/gain/pallas_call | solution.py:307
Async XLA Ops:
  13.5 28.7 %all-to-all-start.1 = ((f32[32,32,128]{2,1,0:T(8,128)}), f32[32,32,128]{2,1,0:T(8,128)S(1)}, u32[]{:S(2)}, u32[]{:S(2)}) async-start(f32[32,32,128]{2,1,0:T(8,128)} %get-tuple-element.8), calls=%async_computation.1 | async-start | bytes 1048576 | tf_op jit(solution)/shard_map/all_to_all | solution.py:260
  24.7 17.5 %copy-start = (s32[4096]{0:T(1024)S(1)}, s32[4096]{0:T(1024)}, u32[]{:S(2)}) copy-start(s32[4096]{0:T(1024)} %param.8) | copy-start | bytes 49156

commit v4 on v3

--- a/solution.py
+++ b/solution.py
@@ -15,7 +15,6 @@
 F32 = jnp.float32
 CHUNK = 512
 GROUP = 2
-UNROLL = 4
 
 
 def iota(shape, dim):
@@ -152,7 +151,7 @@
     zero = jnp.zeros((), BF)
     half = iota((shards, LANES), 1) < LANES // 2
 
-    def some_features(g, _):
+    def some_features(g):
         acc = None
         for c in range(length // CHUNK):
             cols = pl.ds(c * CHUNK, CHUNK)
@@ -183,12 +182,11 @@
             else:
                 grad = pltpu.roll(grad, LANES // 2, 1)
             sums_buf[:, g * GROUP + j, :] = jnp.where(half, grad, hess)
-        return 0
 
     last = iota((8, LANES), 1) % (LANES // 2) >= LANES // 2 - NODES
 
-    def eight_features(g, _):
-        at = pl.ds(pl.multiple_of(g * 8, 8), 8)
+    def eight_features(g):
+        at = pl.ds(g * 8, 8)
         below = jnp.zeros((8, LANES), F32)
         for k in range(shards):
             block = sums_buf[k, at, :]
@@ -197,15 +195,13 @@
             for shift in (32, 16, 8):
                 step += pltpu.roll(step, LANES - shift, 1)
             below += step
-        return 0
-
-    def both_stages(g, _):
+
+    for g in range(feats // 8):
         for j in range(8 // GROUP):
-            some_features(g * (8 // GROUP) + j, 0)
-        return eight_features(jnp.maximum(g - 1, 0), 0)
-
-    lax.fori_loop(0, feats // 8, both_stages, 0, unroll=UNROLL)
-    eight_features(feats // 8 - 1, 0)
+            some_features(g * (8 // GROUP) + j)
+        if g:
+            eight_features(g - 1)
+    eight_features(feats // 8 - 1)
     final = out_ref[shards - 1, 0:8, :]
     for k in range(shards):
         out_ref[k, feats : feats + 8, :] = final

time: 91.4 us -> 90.3 us (0.988)
  Pallas kernels: 15.4 us -> 14.3 us
    pallas_call x1, Pallas kernels: 11.5 us -> 10.4 us  [shards(): call(hist_kernel, (shape((quarter, LANES), F32), shape((quarter, LANES),...]
where the time goes in v4:
time: 90.3 us; the launch traced here: 89.9 us
  blocking collectives  46.2 us (51%)
  waiting for transfers between devices  15.3 us (17%)
  Pallas kernels  14.3 us (16%)
  starting transfers between devices  11.2 us (12%)
  other arithmetic  2.18 us (2%)
    all_to_all x2, blocking collectives, exchange(): return lax.all_to_all(blocks, axes, 0, 0, tiled=True)  46.2 us
    all_to_all x1, waiting for transfers between devices, exchange(): return lax.all_to_all(blocks, axes, 0, 0, tiled=True)  15.3 us
    all_to_all x1, starting transfers between devices, exchange(): return lax.all_to_all(blocks, axes, 0, 0, tiled=True)  11.2 us
    pallas_call x1, Pallas kernels, shards(): call(hist_kernel, (shape((quarter, LANES), F32), shape((quarter, LANES),...  10.4 us
    convert_element_type x1, other arithmetic, shards(): lo = (bin_index % 8).astype(F32)  2.18 us
  transfers between devices with their start and end apart: 1, of which 1 were waited for; matrix products, arithmetic and copies ran while one was open for 2% of the time, Pallas kernels for 0%

profile of v4, /device:TPU:32, one launch (start us, length us, event | category | flops | bytes accessed | tf_op | source)
XLA Modules:
  0.0 89.9 jit_solution(14412249188780666929)
XLA Ops:
  0.6 1.4 %spread.1 = f32[8,12,128]{2,1,0:T(8,128)} custom-call(f32[4,128]{1,0:T(4,128)} %bitcast.9, s32[4,128]{1,0:T(4,128)} %bitcast.10, s32[4,128]{1,0:T(4,128)} %bitcast.11), custom_call_target="tpu_custom_call" | custom-call | tf_op jit(solution)/shard_map/spread/pallas_call | solution.py:266
  2.0 10.1 %all_to_all.15.got_ref = f32[8,12,128]{2,1,0:T(8,128)S(1)} all-to-all(f32[8,12,128]{2,1,0:T(8,128)} %spread.1), channel_id=1, replica_groups=mesh['row_0'=4,'row_1'=8,'feat_0'=4,'feat_1'=2] {'feat_0','feat_1'}, dimensions={0} | all-to-all | bytes 98304 | tf_op jit(solution)/shard_map/all_to_all | solution.py:256
  12.1 1.4 %risk.1 = (f32[32,32,128]{2,1,0:T(8,128)}, f32[4,32,128]{2,1,0:T(8,128)S(1)}) custom-call(f32[8,12,128]{2,1,0:T(8,128)S(1)} %all_to_all.15.got_ref), custom_call_target="tpu_custom_call" | custom-call | tf_op jit(solution)/shard_map/risk/pallas_call | solution.py:276
  13.5 11.2 %all-to-all-start.1 = ((f32[32,32,128]{2,1,0:T(8,128)}), f32[32,32,128]{2,1,0:T(8,128)S(1)}, u32[]{:S(2)}, u32[]{:S(2)}) async-start(f32[32,32,128]{2,1,0:T(8,128)} %get-tuple-element.8), calls=%async_computation.1 | async-start | bytes 1048576 | tf_op jit(solution)/shard_map/all_to_all | solution.py:256
  24.7 0.0 copy-start
  24.7 2.2 %fusion.1 = (f32[64,4096]{1,0:T(8,128)S(1)}, f32[64,4096]{1,0:T(8,128)S(1)}) fusion(s32[64,4096]{1,0:T(8,128)} %param.9), kind=kLoop, calls=%fused_computation.6 | loop fusion | flops 5505024 | bytes 3145728 | tf_op jit(solution)/shard_map/convert_element_type | solution.py:284
  26.9 15.3 %all-to-all-done.1.got_ref = f32[32,32,128]{2,1,0:T(8,128)S(1)} async-done(((f32[32,32,128]{2,1,0:T(8,128)}), f32[32,32,128]{2,1,0:T(8,128)S(1)}, u32[]{:S(2)}, u32[]{:S(2)}) %all-to-all-start.1) | async-done | bytes 524320 | tf_op jit(solution)/shard_map/all_to_all | solution.py:256
  42.2 0.0 copy-done
  42.2 10.4 %hist.1 = (f32[4,128]{1,0:T(4,128)}, f32[4,128]{1,0:T(4,128)}, f32[32,72,128]{2,1,0:T(8,128)S(1)}) custom-call(f32[32,32,128]{2,1,0:T(8,128)S(1)} %all-to-all-done.1.got_ref, f32[4,32,128]{2,1,0:T(8,128)S(1)} %get-tuple-element.9.own_ref, s32[32,128]{1,0:T(8,128)S(1)} %bitcast.7, f32[64,4096]{1,0:T(8,128)S(1)} %get-tuple-element.14.hi_ref, ...), custom_call_target="tpu_custom_call" | custom-call | tf_op jit(solution)/shard_map/hist/pallas_call | solution.py:285
  52.6 36.1 %all_to_all.16.got_ref = f32[32,72,128]{2,1,0:T(8,128)S(1)} all-to-all(f32[32,72,128]{2,1,0:T(8,128)S(1)} %get-tuple-element.12), channel_id=1, replica_groups=mesh['row_0'=4,'row_1'=8,'feat_0'=4,'feat_1'=2] {'row_0','row_1'}, dimensions={0} | all-to-all | bytes 2359296 | tf_op jit(solution)/shard_map/all_to_all | solution.py:256
  88.8 1.1 %gain.1 = f32[8,8,64]{2,1,0:T(8,128)} custom-call(f32[32,72,128]{2,1,0:T(8,128)S(1)} %all_to_all.16.got_ref), custom_call_target="tpu_custom_call" | custom-call | tf_op jit(solution)/shard_map/gain/pallas_call | solution.py:303
Async XLA Ops:
  13.5 28.7 %all-to-all-start.1 = ((f32[32,32,128]{2,1,0:T(8,128)}), f32[32,32,128]{2,1,0:T(8,128)S(1)}, u32[]{:S(2)}, u32[]{:S(2)}) async-start(f32[32,32,128]{2,1,0:T(8,128)} %get-tuple-element.8), calls=%async_computation.1 | async-start | bytes 1048576 | tf_op jit(solution)/shard_map/all_to_all | solution.py:256
  24.7 17.5 %copy-start = (s32[4096]{0:T(1024)S(1)}, s32[4096]{0:T(1024)}, u32[]{:S(2)}) copy-start(s32[4096]{0:T(1024)} %param.8) | copy-start | bytes 49156

commit v5 on v4

--- a/solution.py
+++ b/solution.py
@@ -190,7 +190,9 @@
         below = jnp.zeros((8, LANES), F32)
         for k in range(shards):
             block = sums_buf[k, at, :]
-            out_ref[k, at, :] = block + below
+            done = block + below
+            out_ref[k, 2 * g] = done[:4]
+            out_ref[k, 2 * g + 1] = done[4:]
             step = jnp.where(last, block, 0.0)
             for shift in (32, 16, 8):
                 step += pltpu.roll(step, LANES - shift, 1)
@@ -202,18 +204,21 @@
         if g:
             eight_features(g - 1)
     eight_features(feats // 8 - 1)
-    final = out_ref[shards - 1, 0:8, :]
+    final = out_ref[shards - 1, 0]
     for k in range(shards):
-        out_ref[k, feats : feats + 8, :] = final
+        out_ref[k, feats // 4] = final
 
 
 def gain_kernel(got_ref, out_ref):
-    shards, feats = got_ref.shape[0], got_ref.shape[1] - 8
-    left = got_ref[0]
-    for k in range(1, shards):
-        left += got_ref[k]
-    total = left[feats : feats + 1, :]
-    left = left[:feats]
+    shards, quads = got_ref.shape[0], got_ref.shape[1]
+    pieces = []
+    for q in range(quads):
+        piece = got_ref[0, q]
+        for k in range(1, shards):
+            piece += got_ref[k, q]
+        pieces.append(piece)
+    total = pieces[-1][0:1, :]
+    left = jnp.concatenate(pieces[:-1], 0)
     last = iota((1, LANES), 1) % (LANES // 2) >= LANES // 2 - NODES
     total = jnp.where(last, total, 0.0)
     for shift in (32, 16, 8):
@@ -287,7 +292,7 @@
         (
             shape((quarter, LANES), F32),
             shape((quarter, LANES), F32),
-            shape((n_row, feats + 8, LANES), F32),
+            shape((n_row, feats // 4 + 1, 4, LANES), F32),
         ),
         5,
         "hist",

time: 90.3 us -> 89.1 us (0.987)
  blocking collectives: 46.2 us -> 44.9 us
    all_to_all x2, blocking collectives: 46.2 us -> 44.9 us  [exchange(): return lax.all_to_all(blocks, axes, 0, 0, tiled=True)]
where the time goes in v5:
time: 89.1 us; the launch traced here: 88.5 us
  blocking collectives  44.9 us (50%)
  waiting for transfers between devices  15.3 us (17%)
  Pallas kernels  14.3 us (16%)
  starting transfers between devices  11.2 us (13%)
  other arithmetic  2.18 us (2%)
    all_to_all x2, blocking collectives, exchange(): return lax.all_to_all(blocks, axes, 0, 0, tiled=True)  44.9 us
    all_to_all x1, waiting for transfers between devices, exchange(): return lax.all_to_all(blocks, axes, 0, 0, tiled=True)  15.3 us
    all_to_all x1, starting transfers between devices, exchange(): return lax.all_to_all(blocks, axes, 0, 0, tiled=True)  11.2 us
    pallas_call x1, Pallas kernels, shards(): call(hist_kernel, (shape((quarter, LANES), F32), shape((quarter, LANES),...  10.4 us
    convert_element_type x1, other arithmetic, shards(): lo = (bin_index % 8).astype(F32)  2.18 us
  transfers between devices with their start and end apart: 1, of which 1 were waited for; matrix products, arithmetic and copies ran while one was open for 2% of the time, Pallas kernels for 0%

profile of v5, /device:TPU:32, one launch (start us, length us, event | category | flops | bytes accessed | tf_op | source)
XLA Modules:
  0.0 88.5 jit_solution(7282063950414542633)
XLA Ops:
  0.6 1.4 %spread.1 = f32[8,12,128]{2,1,0:T(8,128)} custom-call(f32[4,128]{1,0:T(4,128)} %bitcast.9, s32[4,128]{1,0:T(4,128)} %bitcast.10, s32[4,128]{1,0:T(4,128)} %bitcast.11), custom_call_target="tpu_custom_call" | custom-call | tf_op jit(solution)/shard_map/spread/pallas_call | solution.py:271
  2.0 10.1 %all_to_all.15.got_ref = f32[8,12,128]{2,1,0:T(8,128)S(1)} all-to-all(f32[8,12,128]{2,1,0:T(8,128)} %spread.1), channel_id=1, replica_groups=mesh['row_0'=4,'row_1'=8,'feat_0'=4,'feat_1'=2] {'feat_0','feat_1'}, dimensions={0} | all-to-all | bytes 98304 | tf_op jit(solution)/shard_map/all_to_all | solution.py:261
  12.1 1.4 %risk.1 = (f32[32,32,128]{2,1,0:T(8,128)}, f32[4,32,128]{2,1,0:T(8,128)S(1)}) custom-call(f32[8,12,128]{2,1,0:T(8,128)S(1)} %all_to_all.15.got_ref), custom_call_target="tpu_custom_call" | custom-call | tf_op jit(solution)/shard_map/risk/pallas_call | solution.py:281
  13.5 11.2 %all-to-all-start.1 = ((f32[32,32,128]{2,1,0:T(8,128)}), f32[32,32,128]{2,1,0:T(8,128)S(1)}, u32[]{:S(2)}, u32[]{:S(2)}) async-start(f32[32,32,128]{2,1,0:T(8,128)} %get-tuple-element.8), calls=%async_computation.1 | async-start | bytes 1048576 | tf_op jit(solution)/shard_map/all_to_all | solution.py:261
  24.7 0.0 copy-start
  24.7 2.2 %fusion.1 = (f32[64,4096]{1,0:T(8,128)S(1)}, f32[64,4096]{1,0:T(8,128)S(1)}) fusion(s32[64,4096]{1,0:T(8,128)} %param.9), kind=kLoop, calls=%fused_computation.6 | loop fusion | flops 5505024 | bytes 3145728 | tf_op jit(solution)/shard_map/convert_element_type | solution.py:289
  26.9 15.3 %all-to-all-done.1.got_ref = f32[32,32,128]{2,1,0:T(8,128)S(1)} async-done(((f32[32,32,128]{2,1,0:T(8,128)}), f32[32,32,128]{2,1,0:T(8,128)S(1)}, u32[]{:S(2)}, u32[]{:S(2)}) %all-to-all-start.1) | async-done | bytes 524320 | tf_op jit(solution)/shard_map/all_to_all | solution.py:261
  42.2 0.0 copy-done
  42.2 10.4 %hist.1 = (f32[4,128]{1,0:T(4,128)}, f32[4,128]{1,0:T(4,128)}, f32[32,17,4,128]{3,2,1,0:T(4,128)S(1)}) custom-call(f32[32,32,128]{2,1,0:T(8,128)S(1)} %all-to-all-done.1.got_ref, f32[4,32,128]{2,1,0:T(8,128)S(1)} %get-tuple-element.9.own_ref, s32[32,128]{1,0:T(8,128)S(1)} %bitcast.7, f32[64,4096]{1,0:T(8,128)S(1)} %get-tuple-element.14.hi_ref, ...), custom_call_target="tpu_custom_call" | custom-call | tf_op jit(solution)/shard_map/hist/pallas_call | solution.py:290
  52.6 34.8 %all_to_all.16.got_ref = f32[32,17,4,128]{3,2,1,0:T(4,128)S(1)} all-to-all(f32[32,17,4,128]{3,2,1,0:T(4,128)S(1)} %get-tuple-element.12), channel_id=1, replica_groups=mesh['row_0'=4,'row_1'=8,'feat_0'=4,'feat_1'=2] {'row_0','row_1'}, dimensions={0} | all-to-all | bytes 2228224 | tf_op jit(solution)/shard_map/all_to_all | solution.py:261
  87.5 1.1 %gain.1 = f32[8,8,64]{2,1,0:T(8,128)} custom-call(f32[32,17,4,128]{3,2,1,0:T(4,128)S(1)} %all_to_all.16.got_ref), custom_call_target="tpu_custom_call" | custom-call | tf_op jit(solution)/shard_map/gain/pallas_call | solution.py:308
Async XLA Ops:
  13.5 28.7 %all-to-all-start.1 = ((f32[32,32,128]{2,1,0:T(8,128)}), f32[32,32,128]{2,1,0:T(8,128)S(1)}, u32[]{:S(2)}, u32[]{:S(2)}) async-start(f32[32,32,128]{2,1,0:T(8,128)} %get-tuple-element.8), calls=%async_computation.1 | async-start | bytes 1048576 | tf_op jit(solution)/shard_map/all_to_all | solution.py:261
  24.7 17.5 %copy-start = (s32[4096]{0:T(1024)S(1)}, s32[4096]{0:T(1024)}, u32[]{:S(2)}) copy-start(s32[4096]{0:T(1024)} %param.8) | copy-start | bytes 49156

commit v6 on v5

--- a/solution.py
+++ b/solution.py
@@ -13,7 +13,7 @@
 ROW_FEAT = ROW + FEAT
 BF = jnp.bfloat16
 F32 = jnp.float32
-CHUNK = 512
+CHUNK = 1024
 GROUP = 2
 
 

time: 89.1 us -> 89.1 us (level)
  no operation moved by 1% of the time
where the time goes in v6:
time: 89.1 us; the launch traced here: 88.5 us
  blocking collectives  44.9 us (50%)
  waiting for transfers between devices  15.3 us (17%)
  Pallas kernels  14.2 us (16%)
  starting transfers between devices  11.2 us (13%)
  other arithmetic  2.18 us (2%)
    all_to_all x2, blocking collectives, exchange(): return lax.all_to_all(blocks, axes, 0, 0, tiled=True)  44.9 us
    all_to_all x1, waiting for transfers between devices, exchange(): return lax.all_to_all(blocks, axes, 0, 0, tiled=True)  15.3 us
    all_to_all x1, starting transfers between devices, exchange(): return lax.all_to_all(blocks, axes, 0, 0, tiled=True)  11.2 us
    pallas_call x1, Pallas kernels, shards(): call(hist_kernel, (shape((quarter, LANES), F32), shape((quarter, LANES),...  10.3 us
    convert_element_type x1, other arithmetic, shards(): lo = (bin_index % 8).astype(F32)  2.18 us
  transfers between devices with their start and end apart: 1, of which 1 were waited for; matrix products, arithmetic and copies ran while one was open for 2% of the time, Pallas kernels for 0%

profile of v6, /device:TPU:32, one launch (start us, length us, event | category | flops | bytes accessed | tf_op | source)
XLA Modules:
  0.0 88.5 jit_solution(1154619945234896779)
XLA Ops:
  0.6 1.4 %spread.1 = f32[8,12,128]{2,1,0:T(8,128)} custom-call(f32[4,128]{1,0:T(4,128)} %bitcast.9, s32[4,128]{1,0:T(4,128)} %bitcast.10, s32[4,128]{1,0:T(4,128)} %bitcast.11), custom_call_target="tpu_custom_call" | custom-call | tf_op jit(solution)/shard_map/spread/pallas_call | solution.py:271
  2.0 10.1 %all_to_all.15.got_ref = f32[8,12,128]{2,1,0:T(8,128)S(1)} all-to-all(f32[8,12,128]{2,1,0:T(8,128)} %spread.1), channel_id=1, replica_groups=mesh['row_0'=4,'row_1'=8,'feat_0'=4,'feat_1'=2] {'feat_0','feat_1'}, dimensions={0} | all-to-all | bytes 98304 | tf_op jit(solution)/shard_map/all_to_all | solution.py:261
  12.1 1.4 %risk.1 = (f32[32,32,128]{2,1,0:T(8,128)}, f32[4,32,128]{2,1,0:T(8,128)S(1)}) custom-call(f32[8,12,128]{2,1,0:T(8,128)S(1)} %all_to_all.15.got_ref), custom_call_target="tpu_custom_call" | custom-call | tf_op jit(solution)/shard_map/risk/pallas_call | solution.py:281
  13.5 11.2 %all-to-all-start.1 = ((f32[32,32,128]{2,1,0:T(8,128)}), f32[32,32,128]{2,1,0:T(8,128)S(1)}, u32[]{:S(2)}, u32[]{:S(2)}) async-start(f32[32,32,128]{2,1,0:T(8,128)} %get-tuple-element.8), calls=%async_computation.1 | async-start | bytes 1048576 | tf_op jit(solution)/shard_map/all_to_all | solution.py:261
  24.7 0.0 copy-start
  24.7 2.2 %fusion.1 = (f32[64,4096]{1,0:T(8,128)S(1)}, f32[64,4096]{1,0:T(8,128)S(1)}) fusion(s32[64,4096]{1,0:T(8,128)} %param.9), kind=kLoop, calls=%fused_computation.6 | loop fusion | flops 5505024 | bytes 3145728 | tf_op jit(solution)/shard_map/convert_element_type | solution.py:289
  26.9 15.3 %all-to-all-done.1.got_ref = f32[32,32,128]{2,1,0:T(8,128)S(1)} async-done(((f32[32,32,128]{2,1,0:T(8,128)}), f32[32,32,128]{2,1,0:T(8,128)S(1)}, u32[]{:S(2)}, u32[]{:S(2)}) %all-to-all-start.1) | async-done | bytes 524320 | tf_op jit(solution)/shard_map/all_to_all | solution.py:261
  42.2 0.0 copy-done
  42.2 10.3 %hist.1 = (f32[4,128]{1,0:T(4,128)}, f32[4,128]{1,0:T(4,128)}, f32[32,17,4,128]{3,2,1,0:T(4,128)S(1)}) custom-call(f32[32,32,128]{2,1,0:T(8,128)S(1)} %all-to-all-done.1.got_ref, f32[4,32,128]{2,1,0:T(8,128)S(1)} %get-tuple-element.9.own_ref, s32[32,128]{1,0:T(8,128)S(1)} %bitcast.7, f32[64,4096]{1,0:T(8,128)S(1)} %get-tuple-element.14.hi_ref, ...), custom_call_target="tpu_custom_call" | custom-call | tf_op jit(solution)/shard_map/hist/pallas_call | solution.py:290
  52.6 34.8 %all_to_all.16.got_ref = f32[32,17,4,128]{3,2,1,0:T(4,128)S(1)} all-to-all(f32[32,17,4,128]{3,2,1,0:T(4,128)S(1)} %get-tuple-element.12), channel_id=1, replica_groups=mesh['row_0'=4,'row_1'=8,'feat_0'=4,'feat_1'=2] {'row_0','row_1'}, dimensions={0} | all-to-all | bytes 2228224 | tf_op jit(solution)/shard_map/all_to_all | solution.py:261
  87.4 1.1 %gain.1 = f32[8,8,64]{2,1,0:T(8,128)} custom-call(f32[32,17,4,128]{3,2,1,0:T(4,128)S(1)} %all_to_all.16.got_ref), custom_call_target="tpu_custom_call" | custom-call | tf_op jit(solution)/shard_map/gain/pallas_call | solution.py:308
Async XLA Ops:
  13.5 28.7 %all-to-all-start.1 = ((f32[32,32,128]{2,1,0:T(8,128)}), f32[32,32,128]{2,1,0:T(8,128)S(1)}, u32[]{:S(2)}, u32[]{:S(2)}) async-start(f32[32,32,128]{2,1,0:T(8,128)} %get-tuple-element.8), calls=%async_computation.1 | async-start | bytes 1048576 | tf_op jit(solution)/shard_map/all_to_all | solution.py:261
  24.7 17.5 %copy-start = (s32[4096]{0:T(1024)S(1)}, s32[4096]{0:T(1024)}, u32[]{:S(2)}) copy-start(s32[4096]{0:T(1024)} %param.8) | copy-start | bytes 49156
